TPU v7x, 32 devices: a whole 2x2x4 slice. The times are simulated.
32 devices in a mesh: groups: 2 (over y), space: 4 (over z), shot: 4 (over x, core).
Axes of the slice: x: 2, y: 2, z: 4, core: 2. Of those that a mesh axis runs over, the one named last changes fastest.
Arguments:
- wavefields: float32 [8, 2, 2, 64, 16, 256], P(('groups', 'shot'), None, None, 'space'), parts along dimension 0, may hold values from -6 to 6
- velocity: float32 [128, 16, 256], P(('groups', 'space'), 'shot'), parts along dimension 0, may hold values from 0.05 to 0.18
- aperture: int32 [8, 2], P(('groups', 'shot')), parts along dimension 0, may hold values from 0 to 64, as said below
Outputs:
- final_fields: float32 [8, 2, 2, 64, 16, 256], P(('groups', 'shot'), None, None, 'space'), parts along dimension 0
- image: float32 [128, 16, 256], P(('groups', 'space'), 'shot'), parts along dimension 0
There are 2 independent parts, one for each index of `groups`. A program takes and returns all parts, laid end to end along the dimension named above; each array names one. Nothing has to cross between parts.
Inputs may be any that keep to these rules, and one draw needn't show every extreme that they name: Row s holds shot s's aperture [lo, hi): lo below 16 and hi above 48.
All inputs are finite; a program needn't handle non-finite values.
Results may differ from a plain program's by a relative error of at most 0.0003.
Values sent between devices are 32-bit elements; how exact they have to be, the bound alone decides.
A program may use at most 64 MiB of HBM per device.

v0:
```python
import jax
import jax.numpy as jnp
from jax import lax
from jax.sharding import PartitionSpec as P

STEPS = 8


coefficients = (-205.0 / 72.0, 8.0 / 5.0, -1.0 / 5.0, 8.0 / 315.0, -1.0 / 560.0)


def with_halo(cells, sides, width):
    for axis, dim in sides:
        count = lax.axis_size(axis)
        ends = count - 1
        head = lax.slice_in_dim(cells, 0, width, axis=dim)
        tail = lax.slice_in_dim(cells, cells.shape[dim] - width, cells.shape[dim], axis=dim)
        cells = jnp.concatenate(
            [
                lax.ppermute(tail, axis, [(i, (i + 1) % count) for i in range(ends)]),
                cells,
                lax.ppermute(head, axis, [((i + 1) % count, i) for i in range(ends)]),
            ],
            axis=dim,
        )
    return cells


def laplace(padded):
    rows_x = padded.shape[1] - 8
    rows_y = padded.shape[2]
    rows_z = padded.shape[3]
    padded_all = jnp.pad(padded, ((0, 0), (0, 0), (4, 4), (4, 4)))
    center = padded_all[:, 4 : 4 + rows_x, 4 : 4 + rows_y, 4 : 4 + rows_z]
    summed = 3.0 * coefficients[0] * center
    for reach in range(1, 5):
        beside_all = padded_all[:, 4 + reach : 4 + reach + rows_x, 4 : 4 + rows_y, 4 : 4 + rows_z]
        beside_all = (
            beside_all
            + padded_all[:, 4 - reach : 4 - reach + rows_x, 4 : 4 + rows_y, 4 : 4 + rows_z]
        )
        beside_all = (
            beside_all
            + padded_all[:, 4 : 4 + rows_x, 4 + reach : 4 + reach + rows_y, 4 : 4 + rows_z]
        )
        beside_all = (
            beside_all
            + padded_all[:, 4 : 4 + rows_x, 4 - reach : 4 - reach + rows_y, 4 : 4 + rows_z]
        )
        beside_all = (
            beside_all
            + padded_all[:, 4 : 4 + rows_x, 4 : 4 + rows_y, 4 + reach : 4 + reach + rows_z]
        )
        beside_all = (
            beside_all
            + padded_all[:, 4 : 4 + rows_x, 4 : 4 + rows_y, 4 - reach : 4 - reach + rows_z]
        )
        summed = summed + coefficients[reach] * beside_all
    return summed


def aperture_mask(bounds, offset, count):
    global_x = offset + jnp.arange(count, dtype=jnp.int32)
    inside = (global_x >= bounds[0]) & (global_x < bounds[1])
    return inside.astype(jnp.float32)[:, None, None]


def shards(wavefields, velocity, aperture):
    fields = wavefields[0]
    cells_x = fields.shape[2]
    bounds = aperture[0]
    offset = lax.axis_index("space") * cells_x
    speed_sq = lax.all_gather(velocity, "shot", axis=1, tiled=True)
    inside = aperture_mask(bounds, offset, cells_x)
    previous = fields[0]
    current = fields[1]
    image_sum = jnp.zeros(speed_sq.shape, jnp.float32)
    speed_wide = with_halo(speed_sq, (("space", 0),), 4)
    inside_wide = aperture_mask(bounds, offset - 4, cells_x + 8)
    for pair_index in range(STEPS // 2):
        stacked = with_halo(jnp.stack([previous, current]), (("space", 2),), 8)
        previous_wide = stacked[0][:, 4:-4]
        current_full = stacked[1]
        current_wide = current_full[:, 4:-4]
        middle = inside_wide * (
            2.0 * current_wide - previous_wide + speed_wide * laplace(current_full)
        )
        first_step = middle[:, 4:-4]
        image_sum = image_sum + first_step[0] * first_step[1]
        second_step = inside * (2.0 * first_step - current + speed_sq * laplace(middle))
        image_sum = image_sum + second_step[0] * second_step[1]
        previous = first_step
        current = second_step
    image_slab = lax.psum_scatter(image_sum, "shot", scatter_dimension=1, tiled=True) / STEPS
    return (jnp.stack([previous, current])[None], image_slab)


def solution(mesh):
    in_specs = (
        P(("groups", "shot"), None, None, "space", None, None),
        P(("groups", "space"), "shot", None),
        P(("groups", "shot"), None),
    )
    out_specs = (
        P(("groups", "shot"), None, None, "space", None, None),
        P(("groups", "space"), "shot", None),
    )
    return jax.shard_map(shards, mesh=mesh, in_specs=in_specs, out_specs=out_specs, check_vma=False)
```

profile of v0, /device:TPU:0, one launch (start us, length us, event | category | flops | bytes accessed | tf_op | source)
XLA Modules:
  0.0 139.3 jit_solution(11397282518371929591)
XLA Ops:
  9.2 5.8 %collective-permute-start = (f32[2,2,8,16,256]{4,2,3,1,0:T(8,128)S(1)}, f32[2,2,8,16,256]{4,2,3,1,0:T(8,128)}, u32[]{:S(2)}, u32[]{:S(2)}) collective-permute-start(f32[2,2,8,16,256]{4,2,3,1,0:T(8,128)S(1)} %get-tuple-element.18), channel_id=1, source_target_pairs={{0,4},{4,8},{8,12},{1,5},{5,9},{9,13},{2,6},{6,10},{10,14},{3,7},{... | collective-permute-start | bytes 1572872 | tf_op jit(solution)/shard_map/ppermute | solution.py:20
  16.3 5.8 %all_gather.3 = f32[16,16,256]{2,0,1:T(8,128)S(1)} all-gather(f32[16,4,256]{2,0,1:T(8,128)S(1)} %copy.7), channel_id=1, replica_groups=mesh['groups'=2,'space'=4,'shot'=4] {'shot'}, dimensions={1}, use_global_device_ids=true | all-gather | bytes 327680 | tf_op jit(solution)/shard_map/all_gather | solution.py:73
  22.1 4.6 %collective-permute-start.2 = (f32[4,16,256]{2,0,1:T(4,128)S(1)}, f32[4,16,256]{2,0,1:T(4,128)S(1)}, u32[]{:S(2)}, u32[]{:S(2)}) collective-permute-start(f32[4,16,256]{2,0,1:T(4,128)S(1)} %get-tuple-element.30), channel_id=1, source_target_pairs={{0,4},{4,8},{8,12},{1,5},{5,9},{9,13},{2,6},{6,10},{10,14},{3,7},{... | collective-permute-start | bytes 196616 | tf_op jit(solution)/shard_map/ppermute | solution.py:20
  26.7 1.3 collective-permute-start.3
  28.6 1.3 and_convert_fusion
  29.9 1.3 and_convert_fusion.1
  31.2 1.6 %collective-permute-done.3 = f32[4,16,256]{2,0,1:T(4,128)S(1)} collective-permute-done((f32[4,16,256]{2,0,1:T(4,128)S(1)}, f32[4,16,256]{2,0,1:T(4,128)S(1)}, u32[]{:S(2)}, u32[]{:S(2)}) %collective-permute-start.3) | collective-permute-done | bytes 65568 | tf_op jit(solution)/shard_map/ppermute | solution.py:22
  32.9 1.5 %pad_maximum_fusion = f32[2,2,32,16,256]{4,2,3,1,0:T(8,128)S(1)} fusion(f32[2,2,8,16,256]{4,2,3,1,0:T(8,128)} %collective-permute-done.1, f32[1,2,16,16,256]{4,2,3,1,0:T(8,128)S(1)} %get-tuple-element.35, f32[1,2,16,16,256]{4,2,3,1,0:T(8,128)S(1)} %get-tuple-element.34, f32[2,2,8,16,256]{4,2,3,1,0:T(8,128)} %collective-permute-done), kind=kLoop, calls=%fused_computation.128 | loop fusion | flops 1572864 | bytes 4194304 | tf_op jit(solution)/shard_map/concatenate | solution.py:18
  34.7 2.2 %fusion.11 = f32[2,24,16,256]{3,1,2,0:T(8,128)S(1)} fusion(f32[2,32,16,256]{3,1,2,0:T(8,128)S(1)} %get-tuple-element.11, f32[2,32,16,256]{3,1,2,0:T(8,128)S(1)} %get-tuple-element.10, f32[24,16,256]{2,0,1:T(8,128)S(1)} %pad_maximum_fusion.8, f32[24]{0:T(128)S(1)} %and_convert_fusion.1), kind=kLoop, calls=%fused_computation.160 | loop fusion | flops 6684672 | bytes 10093056 | tf_op jit(solution)/shard_map/mul | solution.py:85
  38.4 3.1 %collective-permute-start.4 = (f32[2,2,8,16,256]{4,2,3,1,0:T(8,128)S(1)}, f32[2,2,8,16,256]{4,2,3,1,0:T(8,128)S(1)}, u32[]{:S(2)}, u32[]{:S(2)}) collective-permute-start(f32[2,2,8,16,256]{4,2,3,1,0:T(8,128)S(1)} %get-tuple-element.16), channel_id=1, source_target_pairs={{0,4},{4,8},{8,12},{1,5},{5,9},{9,13},{2,6},{6,10},{10,14},{3,7},{... | collective-permute-start | bytes 1572872 | tf_op jit(solution)/shard_map/ppermute | solution.py:20
  41.5 1.3 collective-permute-start.5
  42.8 9.6 %collective-permute-done.4 = f32[2,2,8,16,256]{4,2,3,1,0:T(8,128)S(1)} collective-permute-done((f32[2,2,8,16,256]{4,2,3,1,0:T(8,128)S(1)}, f32[2,2,8,16,256]{4,2,3,1,0:T(8,128)S(1)}, u32[]{:S(2)}, u32[]{:S(2)}) %collective-permute-start.4) | collective-permute-done | bytes 524320 | tf_op jit(solution)/shard_map/ppermute | solution.py:20
  52.4 4.1 %collective-permute-done.5 = f32[2,2,8,16,256]{4,2,3,1,0:T(8,128)S(1)} collective-permute-done((f32[2,2,8,16,256]{4,2,3,1,0:T(8,128)S(1)}, f32[2,2,8,16,256]{4,2,3,1,0:T(8,128)S(1)}, u32[]{:S(2)}, u32[]{:S(2)}) %collective-permute-start.5) | collective-permute-done | bytes 524320 | tf_op jit(solution)/shard_map/ppermute | solution.py:22
  57.0 2.2 %fusion.38 = f32[2,24,16,256]{3,1,2,0:T(8,128)S(1)} fusion(f32[2,32,16,256]{3,1,2,0:T(8,128)S(1)} %get-tuple-element.9, f32[2,32,16,256]{3,1,2,0:T(8,128)S(1)} %get-tuple-element.8, f32[24,16,256]{2,0,1:T(8,128)S(1)} %pad_maximum_fusion.8, f32[24]{0:T(128)S(1)} %and_convert_fusion.1), kind=kLoop, calls=%fused_computation.187 | loop fusion | flops 6684672 | bytes 10093056 | tf_op jit(solution)/shard_map/mul | solution.py:85
  59.2 1.9 %slice_bitcast_fusion.10 = (f32[1,2,16,16,256]{4,2,3,1,0:T(8,128)}, f32[2,16,16,256]{3,1,2,0:T(8,128)S(1)}) fusion(f32[2,24,16,256]{3,1,2,0:T(8,128)S(1)} %fusion.38, f32[16,16,256]{2,0,1:T(8,128)S(1)} %all_gather.3, f32[2,16,16,256]{3,1,2,0:T(8,128)S(1)} %get-tuple-element.29, f32[16]{0:T(128)S(1)} %and_convert_fusion), kind=kLoop, calls=%fused_computation.413 | loop fusion | flops 4456448 | bytes 7340544 | tf_op jit(solution)/shard_map/stack | solution.py:81
  61.1 1.3 fusion.109
  62.5 3.3 %collective-permute-start.6 = (f32[2,2,8,16,256]{4,2,3,1,0:T(8,128)S(1)}, f32[2,2,8,16,256]{4,2,3,1,0:T(8,128)S(1)}, u32[]{:S(2)}, u32[]{:S(2)}) collective-permute-start(f32[2,2,8,16,256]{4,2,3,1,0:T(8,128)S(1)} %get-tuple-element.14), channel_id=1, source_target_pairs={{0,4},{4,8},{8,12},{1,5},{5,9},{9,13},{2,6},{6,10},{10,14},{3,7},{... | collective-permute-start | bytes 1572872 | tf_op jit(solution)/shard_map/ppermute | solution.py:20
  65.8 1.3 collective-permute-start.7
  67.1 7.9 %collective-permute-done.6 = f32[2,2,8,16,256]{4,2,3,1,0:T(8,128)S(1)} collective-permute-done((f32[2,2,8,16,256]{4,2,3,1,0:T(8,128)S(1)}, f32[2,2,8,16,256]{4,2,3,1,0:T(8,128)S(1)}, u32[]{:S(2)}, u32[]{:S(2)}) %collective-permute-start.6) | collective-permute-done | bytes 524320 | tf_op jit(solution)/shard_map/ppermute | solution.py:20
  75.0 4.8 %collective-permute-done.7 = f32[2,2,8,16,256]{4,2,3,1,0:T(8,128)S(1)} collective-permute-done((f32[2,2,8,16,256]{4,2,3,1,0:T(8,128)S(1)}, f32[2,2,8,16,256]{4,2,3,1,0:T(8,128)S(1)}, u32[]{:S(2)}, u32[]{:S(2)}) %collective-permute-start.7) | collective-permute-done | bytes 524320 | tf_op jit(solution)/shard_map/ppermute | solution.py:22
  80.3 2.2 %fusion.65 = f32[2,24,16,256]{3,1,2,0:T(8,128)S(1)} fusion(f32[2,32,16,256]{3,1,2,0:T(8,128)S(1)} %get-tuple-element.7, f32[2,32,16,256]{3,1,2,0:T(8,128)S(1)} %get-tuple-element.6, f32[24,16,256]{2,0,1:T(8,128)S(1)} %pad_maximum_fusion.8, f32[24]{0:T(128)S(1)} %and_convert_fusion.1), kind=kLoop, calls=%fused_computation.214 | loop fusion | flops 6684672 | bytes 10093056 | tf_op jit(solution)/shard_map/mul | solution.py:85
  82.5 2.8 %slice_bitcast_fusion.9 = (f32[1,2,16,16,256]{4,2,3,1,0:T(8,128)}, f32[2,16,16,256]{3,1,2,0:T(8,128)S(1)}) fusion(f32[2,24,16,256]{3,1,2,0:T(8,128)S(1)} %fusion.65, f32[16,16,256]{2,0,1:T(8,128)} %copy-done.3, f32[2,16,16,256]{3,1,2,0:T(8,128)S(1)} %get-tuple-element.27, f32[16]{0:T(128)S(1)} %and_convert_fusion), kind=kLoop, calls=%fused_computation.412 | loop fusion | flops 4456448 | bytes 7340544 | tf_op jit(solution)/shard_map/stack | solution.py:81
  85.4 1.3 fusion.108
  86.7 3.7 %collective-permute-start.8 = (f32[2,2,8,16,256]{4,2,3,1,0:T(8,128)S(1)}, f32[2,2,8,16,256]{4,2,3,1,0:T(8,128)S(1)}, u32[]{:S(2)}, u32[]{:S(2)}) collective-permute-start(f32[2,2,8,16,256]{4,2,3,1,0:T(8,128)S(1)} %get-tuple-element.12), channel_id=1, source_target_pairs={{0,4},{4,8},{8,12},{1,5},{5,9},{9,13},{2,6},{6,10},{10,14},{3,7},{... | collective-permute-start | bytes 1572872 | tf_op jit(solution)/shard_map/ppermute | solution.py:20
  90.4 1.5 %collective-permute-start.9 = (f32[2,2,8,16,256]{4,2,3,1,0:T(8,128)S(1)}, f32[2,2,8,16,256]{4,2,3,1,0:T(8,128)S(1)}, u32[]{:S(2)}, u32[]{:S(2)}) collective-permute-start(f32[2,2,8,16,256]{4,2,3,1,0:T(8,128)S(1)} %get-tuple-element.13), channel_id=1, source_target_pairs={{4,0},{8,4},{12,8},{5,1},{9,5},{13,9},{6,2},{10,6},{14,10},{7,3},{... | collective-permute-start | bytes 1572872 | tf_op jit(solution)/shard_map/ppermute | solution.py:22
  91.9 7.3 %collective-permute-done.8 = f32[2,2,8,16,256]{4,2,3,1,0:T(8,128)S(1)} collective-permute-done((f32[2,2,8,16,256]{4,2,3,1,0:T(8,128)S(1)}, f32[2,2,8,16,256]{4,2,3,1,0:T(8,128)S(1)}, u32[]{:S(2)}, u32[]{:S(2)}) %collective-permute-start.8) | collective-permute-done | bytes 524320 | tf_op jit(solution)/shard_map/ppermute | solution.py:20
  99.2 4.1 %collective-permute-done.9 = f32[2,2,8,16,256]{4,2,3,1,0:T(8,128)S(1)} collective-permute-done((f32[2,2,8,16,256]{4,2,3,1,0:T(8,128)S(1)}, f32[2,2,8,16,256]{4,2,3,1,0:T(8,128)S(1)}, u32[]{:S(2)}, u32[]{:S(2)}) %collective-permute-start.9) | collective-permute-done | bytes 524320 | tf_op jit(solution)/shard_map/ppermute | solution.py:22
  104.6 2.1 %fusion.92 = f32[2,24,16,256]{3,1,2,0:T(8,128)S(1)} fusion(f32[2,32,16,256]{3,1,2,0:T(8,128)S(1)} %get-tuple-element.5, f32[2,32,16,256]{3,1,2,0:T(8,128)S(1)} %get-tuple-element.4, f32[24,16,256]{2,0,1:T(8,128)S(1)} %copy-done.6, f32[24]{0:T(128)S(1)} %and_convert_fusion.1), kind=kLoop, calls=%fused_computation.241 | loop fusion | flops 6684672 | bytes 10093056 | tf_op jit(solution)/shard_map/mul | solution.py:85
  106.7 3.1 %slice_bitcast_fusion.8 = (f32[1,2,16,16,256]{4,2,3,1,0:T(8,128)}, f32[2,16,16,256]{3,1,2,0:T(8,128)}) fusion(f32[2,24,16,256]{3,1,2,0:T(8,128)S(1)} %fusion.92, f32[16,16,256]{2,0,1:T(8,128)S(1)} %copy-done.4, f32[2,16,16,256]{3,1,2,0:T(8,128)} %copy-done.2, f32[16]{0:T(128)S(1)} %and_convert_fusion), kind=kLoop, calls=%fused_computation.411 | loop fusion | flops 4456448 | bytes 7340544 | tf_op jit(solution)/shard_map/stack | solution.py:95
  109.8 2.7 %fusion.221 = f32[16,16,256]{2,0,1:T(8,128)} fusion(f32[2,16,16,256]{3,1,2,0:T(8,128)} %get-tuple-element.23, f32[2,24,16,256]{3,1,2,0:T(8,128)S(1)} %fusion.92, f32[2,16,16,256]{3,1,2,0:T(8,128)} %copy-done.2, f32[2,24,16,256]{3,1,2,0:T(8,128)S(1)} %fusion.65, f32[2,16,16,256]{3,1,2,0:T(8,128)} %copy-done.1, f32[2,24,16,256]{3,1,2,0:T(8,128)S(1)} %fusion.38, ...), kind=kLoop, calls=%fused_computation.419 | loop fusion | flops 983040 | bytes 4456448 | tf_op jit(solution)/shard_map/add | solution.py:91
  113.8 1.6 %copy.8 = f32[1,2,2,16,16,256]{5,4,3,2,1,0:T(8,128)} copy(f32[1,2,2,16,16,256]{5,3,4,2,1,0:T(8,128)S(1)} %maximum_bitcast_fusion) | data formatting | bytes 2097152
  115.4 15.5 %reduce-scatter.2.cloned.1.call-done = f32[16,4,256]{2,0,1:T(8,128)} async-done(((f32[16,16,256]{2,0,1:T(8,128)}), f32[16,4,256]{2,0,1:T(8,128)}) %reduce-scatter.2.cloned.1.call-update) | async-done | bytes 65552 | tf_op jit(solution)/shard_map/reduce_scatter | solution.py:94
  (47 shorter events, 10.5 us)
Async XLA Ops:
  7.2 123.8 %reduce-scatter.2.cloned.1.call-start = ((), (), s32[]{:S(2)}) async-start(), calls=%async_computation.1 | async-start | bytes 327680 | tf_op jit(solution)/shard_map/reduce_scatter | solution.py:94
  8.5 7.8 %copy-start.9 = (f32[16,4,256]{2,1,0:T(4,128)S(1)}, f32[16,4,256]{2,1,0:T(4,128)}, u32[]{:S(2)}) copy-start(f32[16,4,256]{2,1,0:T(4,128)} %param.4) | copy-start | bytes 196612
  8.5 19.5 %copy-start.10 = (s32[1,2]{1,0:T(1,128)S(1)}, s32[1,2]{1,0:T(1,128)}, u32[]{:S(2)}) copy-start(s32[1,2]{1,0:T(1,128)} %param.5) | copy-start | bytes 28
  9.2 23.7 %collective-permute-start = (f32[2,2,8,16,256]{4,2,3,1,0:T(8,128)S(1)}, f32[2,2,8,16,256]{4,2,3,1,0:T(8,128)}, u32[]{:S(2)}, u32[]{:S(2)}) collective-permute-start(f32[2,2,8,16,256]{4,2,3,1,0:T(8,128)S(1)} %get-tuple-element.18), channel_id=1, source_target_pairs={{0,4},{4,8},{8,12},{1,5},{5,9},{9,13},{2,6},{6,10},{10,14},{3,7},{... | collective-permute-start | bytes 1572872 | tf_op jit(solution)/shard_map/ppermute | solution.py:20
  15.0 17.9 %collective-permute-start.1 = (f32[2,2,8,16,256]{4,2,3,1,0:T(8,128)S(1)}, f32[2,2,8,16,256]{4,2,3,1,0:T(8,128)}, u32[]{:S(2)}, u32[]{:S(2)}) collective-permute-start(f32[2,2,8,16,256]{4,2,3,1,0:T(8,128)S(1)} %get-tuple-element.19), channel_id=1, source_target_pairs={{4,0},{8,4},{12,8},{5,1},{9,5},{13,9},{6,2},{10,6},{14,10},{7,3},{... | collective-permute-start | bytes 1572872 | tf_op jit(solution)/shard_map/ppermute | solution.py:22
  22.1 37.1 %copy-start.3 = (f32[16,16,256]{2,0,1:T(8,128)}, f32[16,16,256]{2,0,1:T(8,128)S(1)}, u32[]{:S(2)}) copy-start(f32[16,16,256]{2,0,1:T(8,128)S(1)} %all_gather.3) | copy-start | bytes 786436
  22.1 9.1 %collective-permute-start.2 = (f32[4,16,256]{2,0,1:T(4,128)S(1)}, f32[4,16,256]{2,0,1:T(4,128)S(1)}, u32[]{:S(2)}, u32[]{:S(2)}) collective-permute-start(f32[4,16,256]{2,0,1:T(4,128)S(1)} %get-tuple-element.30), channel_id=1, source_target_pairs={{0,4},{4,8},{8,12},{1,5},{5,9},{9,13},{2,6},{6,10},{10,14},{3,7},{... | collective-permute-start | bytes 196616 | tf_op jit(solution)/shard_map/ppermute | solution.py:20
  26.7 6.2 %collective-permute-start.3 = (f32[4,16,256]{2,0,1:T(4,128)S(1)}, f32[4,16,256]{2,0,1:T(4,128)S(1)}, u32[]{:S(2)}, u32[]{:S(2)}) collective-permute-start(f32[4,16,256]{2,0,1:T(4,128)S(1)} %get-tuple-element.31), channel_id=1, source_target_pairs={{4,0},{8,4},{12,8},{5,1},{9,5},{13,9},{6,2},{10,6},{14,10},{7,3},{... | collective-permute-start | bytes 196616 | tf_op jit(solution)/shard_map/ppermute | solution.py:22
  32.9 47.4 %copy-start.5 = (f32[24,16,256]{2,0,1:T(8,128)}, f32[24,16,256]{2,0,1:T(8,128)S(1)}, u32[]{:S(2)}) copy-start(f32[24,16,256]{2,0,1:T(8,128)S(1)} %pad_maximum_fusion.8) | copy-start | bytes 1179652
  38.3 21.0 %copy-start = (f32[2,16,16,256]{3,1,2,0:T(8,128)}, f32[2,16,16,256]{3,1,2,0:T(8,128)S(1)}, u32[]{:S(2)}) copy-start(f32[2,16,16,256]{3,1,2,0:T(8,128)S(1)} %get-tuple-element.29) | copy-start | bytes 1572868
  38.4 14.0 %collective-permute-start.4 = (f32[2,2,8,16,256]{4,2,3,1,0:T(8,128)S(1)}, f32[2,2,8,16,256]{4,2,3,1,0:T(8,128)S(1)}, u32[]{:S(2)}, u32[]{:S(2)}) collective-permute-start(f32[2,2,8,16,256]{4,2,3,1,0:T(8,128)S(1)} %get-tuple-element.16), channel_id=1, source_target_pairs={{0,4},{4,8},{8,12},{1,5},{5,9},{9,13},{2,6},{6,10},{10,14},{3,7},{... | collective-permute-start | bytes 1572872 | tf_op jit(solution)/shard_map/ppermute | solution.py:20
  41.5 15.0 %collective-permute-start.5 = (f32[2,2,8,16,256]{4,2,3,1,0:T(8,128)S(1)}, f32[2,2,8,16,256]{4,2,3,1,0:T(8,128)S(1)}, u32[]{:S(2)}, u32[]{:S(2)}) collective-permute-start(f32[2,2,8,16,256]{4,2,3,1,0:T(8,128)S(1)} %get-tuple-element.17), channel_id=1, source_target_pairs={{4,0},{8,4},{12,8},{5,1},{9,5},{13,9},{6,2},{10,6},{14,10},{7,3},{... | collective-permute-start | bytes 1572872 | tf_op jit(solution)/shard_map/ppermute | solution.py:22
  61.1 21.4 %copy-start.1 = (f32[2,16,16,256]{3,1,2,0:T(8,128)}, f32[2,16,16,256]{3,1,2,0:T(8,128)S(1)}, u32[]{:S(2)}) copy-start(f32[2,16,16,256]{3,1,2,0:T(8,128)S(1)} %get-tuple-element.27) | copy-start | bytes 1572868
  61.1 18.7 %copy-start.7 = (f32[1,2,16,16,256]{4,2,3,1,0:T(8,128)S(1)}, f32[1,2,16,16,256]{4,2,3,1,0:T(8,128)}, u32[]{:S(2)}) copy-start(f32[1,2,16,16,256]{4,2,3,1,0:T(8,128)} %get-tuple-element.26) | copy-start | bytes 1572868
  62.5 12.6 %collective-permute-start.6 = (f32[2,2,8,16,256]{4,2,3,1,0:T(8,128)S(1)}, f32[2,2,8,16,256]{4,2,3,1,0:T(8,128)S(1)}, u32[]{:S(2)}, u32[]{:S(2)}) collective-permute-start(f32[2,2,8,16,256]{4,2,3,1,0:T(8,128)S(1)} %get-tuple-element.14), channel_id=1, source_target_pairs={{0,4},{4,8},{8,12},{1,5},{5,9},{9,13},{2,6},{6,10},{10,14},{3,7},{... | collective-permute-start | bytes 1572872 | tf_op jit(solution)/shard_map/ppermute | solution.py:20
  65.8 14.1 %collective-permute-start.7 = (f32[2,2,8,16,256]{4,2,3,1,0:T(8,128)S(1)}, f32[2,2,8,16,256]{4,2,3,1,0:T(8,128)S(1)}, u32[]{:S(2)}, u32[]{:S(2)}) collective-permute-start(f32[2,2,8,16,256]{4,2,3,1,0:T(8,128)S(1)} %get-tuple-element.15), channel_id=1, source_target_pairs={{4,0},{8,4},{12,8},{5,1},{9,5},{13,9},{6,2},{10,6},{14,10},{7,3},{... | collective-permute-start | bytes 1572872 | tf_op jit(solution)/shard_map/ppermute | solution.py:22
  85.4 18.2 %copy-start.2 = (f32[2,16,16,256]{3,1,2,0:T(8,128)}, f32[2,16,16,256]{3,1,2,0:T(8,128)S(1)}, u32[]{:S(2)}) copy-start(f32[2,16,16,256]{3,1,2,0:T(8,128)S(1)} %get-tuple-element.25) | copy-start | bytes 1572868
  85.4 18.0 %copy-start.8 = (f32[1,2,16,16,256]{4,2,3,1,0:T(8,128)S(1)}, f32[1,2,16,16,256]{4,2,3,1,0:T(8,128)}, u32[]{:S(2)}) copy-start(f32[1,2,16,16,256]{4,2,3,1,0:T(8,128)} %get-tuple-element.24) | copy-start | bytes 1572868
  86.7 12.5 %collective-permute-start.8 = (f32[2,2,8,16,256]{4,2,3,1,0:T(8,128)S(1)}, f32[2,2,8,16,256]{4,2,3,1,0:T(8,128)S(1)}, u32[]{:S(2)}, u32[]{:S(2)}) collective-permute-start(f32[2,2,8,16,256]{4,2,3,1,0:T(8,128)S(1)} %get-tuple-element.12), channel_id=1, source_target_pairs={{0,4},{4,8},{8,12},{1,5},{5,9},{9,13},{2,6},{6,10},{10,14},{3,7},{... | collective-permute-start | bytes 1572872 | tf_op jit(solution)/shard_map/ppermute | solution.py:20
  90.4 13.0 %collective-permute-start.9 = (f32[2,2,8,16,256]{4,2,3,1,0:T(8,128)S(1)}, f32[2,2,8,16,256]{4,2,3,1,0:T(8,128)S(1)}, u32[]{:S(2)}, u32[]{:S(2)}) collective-permute-start(f32[2,2,8,16,256]{4,2,3,1,0:T(8,128)S(1)} %get-tuple-element.13), channel_id=1, source_target_pairs={{4,0},{8,4},{12,8},{5,1},{9,5},{13,9},{6,2},{10,6},{14,10},{7,3},{... | collective-permute-start | bytes 1572872 | tf_op jit(solution)/shard_map/ppermute | solution.py:22
  103.6 1.0 copy-start.6
  104.5 2.1 %copy-start.4 = (f32[16,16,256]{2,0,1:T(8,128)S(1)}, f32[16,16,256]{2,0,1:T(8,128)}, u32[]{:S(2)}) copy-start(f32[16,16,256]{2,0,1:T(8,128)} %copy-done.3) | copy-start | bytes 786436
Sparse Core Ops, SparseCore 0:
  112.6 18.2 reduce-scatter.1
where the time goes:
time: 140 us; the launch traced here: 139 us
  waiting for transfers between devices  55.2 us (39%)
  other arithmetic  30.3 us (22%)
  starting transfers between devices  27.1 us (19%)
  between operations  14.4 us (10%)
  local copies, waits for them, and re-layouts  6.5 us (5%)
  blocking collectives  5.78 us (4%)
    ppermute x5, waiting for transfers between devices, with_halo(): lax.ppermute(tail, axis, [(i, (i + 1) % count) for i in range(ends)])  24.9 us
    ppermute x5, starting transfers between devices, with_halo(): lax.ppermute(tail, axis, [(i, (i + 1) % count) for i in range(ends)])  20.4 us
    reduce_scatter x1, waiting for transfers between devices, shards(): lax.psum_scatter(image_sum, 'shot', scatter_dimension=1, tiled=True) / STEPS  15.5 us
    ppermute x5, waiting for transfers between devices, with_halo(): lax.ppermute(head, axis, [((i + 1) % count, i) for i in range(ends)])  14.8 us
    another operation x7, other arithmetic, shards(): stacked = with_halo(jnp.stack([previous, current]), (('space', 2),), 8)  8.86 us
    mul x4, other arithmetic, shards(): inside_wide * (2.0 * current_wide - previous_wide + speed_wide * laplace(...  8.75 us
    ppermute x5, starting transfers between devices, with_halo(): lax.ppermute(head, axis, [((i + 1) % count, i) for i in range(ends)])  6.63 us
    all_gather x1, blocking collectives, shards(): speed_sq = lax.all_gather(velocity, 'shot', axis=1, tiled=True)  5.78 us
  transfers between devices with their start and end apart: 11, of which 8 were waited for; matrix products, arithmetic and copies ran while one was open for 4% of the time, Pallas kernels for 0%

commit v1 on v0

v1 whole, which is shorter than its diff:
```python
import functools

import jax
import jax.numpy as jnp
import numpy as np
from jax import lax
from jax.experimental import pallas as pl
from jax.experimental.pallas import tpu as pltpu
from jax.sharding import PartitionSpec as P

STEPS = 8
REACH = 4


coefficients = (-205.0 / 72.0, 8.0 / 5.0, -1.0 / 5.0, 8.0 / 315.0, -1.0 / 560.0)


def band(size):
    matrix = np.zeros((size, size), np.float32)
    for reach in range(1, REACH + 1):
        matrix += np.float32(coefficients[reach]) * (
            np.eye(size, k=reach, dtype=np.float32) + np.eye(size, k=-reach, dtype=np.float32)
        )
    return matrix


def split(matrix, axis):
    high = matrix.astype(jnp.bfloat16)
    low = (matrix - high.astype(np.float32)).astype(jnp.bfloat16)
    return np.concatenate([high, high, low], axis=axis)


def kernel(
    left_ref, right_ref, waves, velocity, aperture, out, image,
    halo, speeds, speed, inside, lap, total, parts, arrived,
    halo_send, halo_recv, speed_send, speed_recv, part_send, part_recv, local_sem,
):
    space = lax.axis_index("space")
    spaces = lax.axis_size("space")
    shot = lax.axis_index("shot")
    shots = lax.axis_size("shot")
    cells_x, rows_y, rows_z = out.shape[2:]
    slab = velocity.shape[1]
    flat = (cells_x * rows_y, rows_z)
    has_left = space > 0
    has_right = space < spaces - 1

    load = pltpu.make_async_copy(waves, out, local_sem.at[0])
    load.start()
    own_speed = pltpu.make_async_copy(velocity, speeds.at[shot], local_sem.at[1])
    own_speed.start()

    barrier = pltpu.get_barrier_semaphore()

    @pl.when(has_left)
    def _():
        pl.semaphore_signal(barrier, inc=1, device_id={"space": space - 1}, device_id_type=pl.DeviceIdType.MESH)

    @pl.when(has_right)
    def _():
        pl.semaphore_signal(barrier, inc=1, device_id={"space": space + 1}, device_id_type=pl.DeviceIdType.MESH)

    for ahead in range(1, shots):
        peer = lax.rem(shot + ahead, shots)
        pl.semaphore_signal(barrier, inc=1, device_id={"shot": peer}, device_id_type=pl.DeviceIdType.MESH)
    pl.semaphore_wait(barrier, shots - 1 + jnp.where(has_left, 1, 0) + jnp.where(has_right, 1, 0))

    def to_right(source, slot, field):
        return pltpu.make_async_remote_copy(
            source.at[field, cells_x - REACH : cells_x],
            halo.at[slot, field, 0],
            halo_send.at[slot, field, 0],
            halo_recv.at[slot, field, 0],
            device_id={"space": space + 1},
            device_id_type=pl.DeviceIdType.MESH,
        )

    def to_left(source, slot, field):
        return pltpu.make_async_remote_copy(
            source.at[field, 0:REACH],
            halo.at[slot, field, 1],
            halo_send.at[slot, field, 1],
            halo_recv.at[slot, field, 1],
            device_id={"space": space - 1},
            device_id_type=pl.DeviceIdType.MESH,
        )

    def send(source, slot, field):
        @pl.when(has_right)
        def _():
            to_right(source, slot, field).start()

        @pl.when(has_left)
        def _():
            to_left(source, slot, field).start()

    def sent(source, slot, field):
        @pl.when(has_right)
        def _():
            to_right(source, slot, field).wait_send()

        @pl.when(has_left)
        def _():
            to_left(source, slot, field).wait_send()

    def received(source, slot, field):
        @pl.when(has_left)
        def _():
            to_right(source, slot, field).wait_recv()

        @pl.when(has_right)
        def _():
            to_left(source, slot, field).wait_recv()

    send(waves.at[1], 0, 0)
    send(waves.at[1], 0, 1)

    speed_copies = []
    for ahead in range(1, shots):
        peer = lax.rem(shot + ahead, shots)
        copy = pltpu.make_async_remote_copy(
            velocity,
            speeds.at[shot],
            speed_send.at[ahead - 1],
            speed_recv.at[ahead - 1],
            device_id={"shot": peer},
            device_id_type=pl.DeviceIdType.MESH,
        )
        copy.start()
        speed_copies.append(copy)

    @pl.when(jnp.logical_not(has_left))
    def _():
        halo[:, :, 0] = jnp.zeros((STEPS, 2, REACH, rows_y, rows_z), jnp.float32)

    @pl.when(jnp.logical_not(has_right))
    def _():
        halo[:, :, 1] = jnp.zeros((STEPS, 2, REACH, rows_y, rows_z), jnp.float32)

    total[...] = jnp.zeros(total.shape, jnp.float32)
    global_x = space * cells_x + lax.broadcasted_iota(jnp.int32, inside.shape, 0)
    within = (global_x >= aperture[0, 0]) & (global_x < aperture[0, 1])
    inside[...] = jnp.where(within, 1.0, 0.0)

    load.wait()
    own_speed.wait()
    for copy in speed_copies:
        copy.wait()
    for index in range(shots):
        rows = slice(index * slab, (index + 1) * slab)
        speed[:, rows, :] = speeds[index]
    speed[...] = speed[...] * inside[...]

    def spread(now, field):
        cells = out[now, field].reshape(flat)
        high = cells.astype(jnp.bfloat16)
        low = (cells - high.astype(jnp.float32)).astype(jnp.bfloat16)
        lap[...] = (
            jnp.dot(left_ref[...], jnp.concatenate([high, low, high], axis=0), preferred_element_type=jnp.float32)
            + jnp.dot(jnp.concatenate([high, low, high], axis=1), right_ref[...], preferred_element_type=jnp.float32)
            + (3.0 * coefficients[0]) * cells
        ).reshape(lap.shape)

    def advance(now, then, field, start, stop, beside=None):
        cells = slice(start, stop)
        summed = lap[cells]
        if beside is not None:
            summed = summed + beside
        following = (
            inside[cells] * (2.0 * out[now, field, cells] - out[then, field, cells])
            + speed[cells] * summed
        )
        out[then, field, cells] = following
        if field == 1:
            total[cells] = total[cells] + out[then, 0, cells] * following

    def step(index, carry):
        then = lax.rem(index, 2)
        now = 1 - then
        for field in range(2):
            spread(now, field)

            @pl.when(index > 1)
            def _():
                sent(out.at[then], index - 1, field)

            @pl.when(index == 1)
            def _():
                sent(waves.at[1], 0, field)

            advance(now, then, field, REACH, cells_x - REACH)
            received(out.at[now], index, field)
            for cell in range(REACH):
                beside = sum(
                    coefficients[cell + REACH - layer] * halo[index, field, 0, layer]
                    for layer in range(cell, REACH)
                )
                advance(now, then, field, cell, cell + 1, beside[None])
                beside = sum(
                    coefficients[REACH + layer - cell] * halo[index, field, 1, layer]
                    for layer in range(cell + 1)
                )
                at = cells_x - REACH + cell
                advance(now, then, field, at, at + 1, beside[None])

            @pl.when(index < STEPS - 1)
            def _():
                send(out.at[then], index + 1, field)

        return carry

    lax.fori_loop(0, STEPS, step, 0)

    for index in range(shots):
        rows = slice(index * slab, (index + 1) * slab)
        parts[index] = total[:, rows, :]
    part_copies = []
    for ahead in range(1, shots):
        peer = lax.rem(shot + ahead, shots)
        copy = pltpu.make_async_remote_copy(
            parts.at[peer],
            arrived.at[ahead - 1],
            part_send.at[ahead - 1],
            part_recv.at[ahead - 1],
            device_id={"shot": peer},
            device_id_type=pl.DeviceIdType.MESH,
        )
        copy.start()
        part_copies.append(copy)
    for field in range(2):
        sent(out.at[(STEPS - 2) % 2], STEPS - 1, field)
    summed = parts[shot]
    for ahead in range(1, shots):
        part_copies[ahead - 1].wait()
        summed = summed + arrived[ahead - 1]
    image[...] = summed / STEPS


def shards(wavefields, velocity, aperture):
    fields = wavefields[0]
    cells_x, rows_y, rows_z = fields.shape[2:]
    shots = lax.axis_size("shot")
    slab = velocity.shape[1]
    left = split(
        np.kron(band(cells_x), np.eye(rows_y, dtype=np.float32))
        + np.kron(np.eye(cells_x, dtype=np.float32), band(rows_y)),
        1,
    )
    right = split(band(rows_z), 0)
    grid = (cells_x, rows_y, rows_z)
    vmem = pl.BlockSpec(memory_space=pltpu.VMEM)
    anywhere = pl.BlockSpec(memory_space=pl.ANY)
    finals, image = pl.pallas_call(
        kernel,
        out_shape=(
            jax.ShapeDtypeStruct(fields.shape, jnp.float32),
            jax.ShapeDtypeStruct(velocity.shape, jnp.float32),
        ),
        in_specs=[vmem, vmem, anywhere, anywhere, pl.BlockSpec(memory_space=pltpu.SMEM)],
        out_specs=(vmem, vmem),
        scratch_shapes=[
            pltpu.VMEM((STEPS, 2, 2, REACH, rows_y, rows_z), jnp.float32),
            pltpu.VMEM((shots,) + velocity.shape, jnp.float32),
            pltpu.VMEM(grid, jnp.float32),
            pltpu.VMEM(grid, jnp.float32),
            pltpu.VMEM(grid, jnp.float32),
            pltpu.VMEM(grid, jnp.float32),
            pltpu.VMEM((shots,) + velocity.shape, jnp.float32),
            pltpu.VMEM((shots - 1,) + velocity.shape, jnp.float32),
            pltpu.SemaphoreType.DMA((STEPS, 2, 2)),
            pltpu.SemaphoreType.DMA((STEPS, 2, 2)),
            pltpu.SemaphoreType.DMA((shots - 1,)),
            pltpu.SemaphoreType.DMA((shots - 1,)),
            pltpu.SemaphoreType.DMA((shots - 1,)),
            pltpu.SemaphoreType.DMA((shots - 1,)),
            pltpu.SemaphoreType.DMA((2,)),
        ],
        compiler_params=pltpu.CompilerParams(collective_id=0, has_side_effects=True),
    )(jnp.asarray(left), jnp.asarray(right), fields, velocity, aperture)
    return finals[None], image


def solution(mesh):
    in_specs = (
        P(("groups", "shot"), None, None, "space", None, None),
        P(("groups", "space"), "shot", None),
        P(("groups", "shot"), None),
    )
    out_specs = (
        P(("groups", "shot"), None, None, "space", None, None),
        P(("groups", "space"), "shot", None),
    )
    return jax.shard_map(shards, mesh=mesh, in_specs=in_specs, out_specs=out_specs, check_vma=False)
```

time: 140 us -> 46.5 us (0.33)
  waiting for transfers between devices: 55.2 us -> 0 us
  Pallas kernels: 0 us -> 42.7 us
  other arithmetic: 30.3 us -> 0 us
  starting transfers between devices: 27.1 us -> 0 us
  between operations: 14.4 us -> 0.65 us
  blocking collectives: 5.78 us -> 0 us
  local copies, waits for them, and re-layouts: 6.5 us -> 2.93 us
    pallas_call x0 -> x1, Pallas kernels: none -> 42.7 us  [shards(): pl.pallas_call(kernel, out_shape=(jax.ShapeDtypeStruct(fields.shape, jnp....]
    ppermute x10 -> x0, waiting for transfers between devices: 39.6 us -> none  [the longest x5 24.9 us: with_halo(): lax.ppermute(tail, axis, [(i, (i + 1) % count) for i in range(ends)])]
    ppermute x10 -> x0, starting transfers between devices: 27.1 us -> none  [the longest x5 20.4 us: with_halo(): lax.ppermute(tail, axis, [(i, (i + 1) % count) for i in range(ends)])]
    reduce_scatter x1 -> x0, waiting for transfers between devices: 15.5 us -> none  [shards(): lax.psum_scatter(image_sum, 'shot', scatter_dimension=1, tiled=True) / STEPS]
    another operation x8 -> x0, other arithmetic: 11.9 us -> none  [the longest x7 8.86 us: shards(): stacked = with_halo(jnp.stack([previous, current]), (('space', 2),), 8)]
    mul x4 -> x0, other arithmetic: 8.75 us -> none  [shards(): inside_wide * (2.0 * current_wide - previous_wide + speed_wide * laplace(...]
    all_gather x1 -> x0, blocking collectives: 5.78 us -> none  [shards(): speed_sq = lax.all_gather(velocity, 'shot', axis=1, tiled=True)]
    add x1 -> x0, other arithmetic: 2.72 us -> none  [shards(): image_sum = image_sum + second_step[0] * second_step[1]]
  transfers between devices with their start and end apart: 11 -> 0, of which waited for: 8 -> 0; matrix products, arithmetic and copies ran while one was open for 4% -> 0% of each run, Pallas kernels for 0% -> 0%
where the time goes in v1:
time: 46.5 us; the launch traced here: 46.3 us
  Pallas kernels  42.7 us (92%)
  local copies, waits for them, and re-layouts  2.93 us (6%)
  between operations  0.65 us (1%)
    pallas_call x1, Pallas kernels, shards(): pl.pallas_call(kernel, out_shape=(jax.ShapeDtypeStruct(fields.shape, jnp....  42.7 us
    unnamed x4, local copies, waits for them, and re-layouts  2.93 us

profile of v1, /device:TPU:0, one launch (start us, length us, event | category | flops | bytes accessed | tf_op | source)
XLA Modules:
  0.0 46.3 jit_solution(11408755986330552571)
XLA Ops:
  0.6 42.7 %shard_map.68 = (f32[2,2,16,16,256]{4,3,2,1,0:T(8,128)}, f32[16,4,256]{2,1,0:T(4,128)}) custom-call(bf16[256,768]{1,0:T(8,128)(2,1)} %constant.4.clone.left_ref, bf16[768,256]{1,0:T(8,128)(2,1)} %constant.5.clone.right_ref, f32[2,2,16,16,256]{4,3,2,1,0:T(8,128)} %bitcast.2, f32[16,4,256]{2,1,0:T(4,128)} %velocity.1, s32[1,2]{1,0:T(1,128)} %aperture.1), custom_call_target="tpu_custom_call" | custom-call | tf_op jit(solution)/shard_map/pallas_call | solution.py:253
  43.3 0.0 copy-start
  43.3 2.3 %copy.9 = f32[1,2,2,16,16,256]{5,4,3,2,1,0:T(8,128)} copy(f32[1,2,2,16,16,256]{5,4,3,2,1,0:T(8,128)} %bitcast.3) | data formatting | bytes 2097152
  45.6 0.0 copy-done
  45.6 0.6 %copy.10 = f32[16,4,256]{2,1,0:T(4,128)} copy(f32[16,4,256]{2,1,0:T(4,128)S(1)} %copy-done) | data formatting | bytes 131072
Async XLA Ops:
  43.3 2.3 %copy-start = (f32[16,4,256]{2,1,0:T(4,128)S(1)}, f32[16,4,256]{2,1,0:T(4,128)}, u32[]{:S(2)}) copy-start(f32[16,4,256]{2,1,0:T(4,128)} %get-tuple-element.9) | copy-start | bytes 196612

commit v2 on v1

v2 whole, which is shorter than its diff:
```python
import functools

import jax
import jax.numpy as jnp
import numpy as np
from jax import lax
from jax.experimental import pallas as pl
from jax.experimental.pallas import tpu as pltpu
from jax.sharding import PartitionSpec as P

STEPS = 8
REACH = 4


coefficients = (-205.0 / 72.0, 8.0 / 5.0, -1.0 / 5.0, 8.0 / 315.0, -1.0 / 560.0)


def band(size):
    matrix = np.zeros((size, size), np.float32)
    for reach in range(1, REACH + 1):
        matrix += np.float32(coefficients[reach]) * (
            np.eye(size, k=reach, dtype=np.float32) + np.eye(size, k=-reach, dtype=np.float32)
        )
    return matrix


def split(matrix, axis):
    high = matrix.astype(jnp.bfloat16)
    low = (matrix - high.astype(np.float32)).astype(jnp.bfloat16)
    return np.concatenate([high, high, low], axis=axis)


def kernel(
    left, right, waves, velocity, aperture, finals, image,
    left_ref, right_ref, out, halo, speeds, speed, inside, lap, total,
    middle, middle_arrived, edges, edges_arrived,
    halo_send, halo_recv, speed_send, speed_recv, part_send, part_recv, local_sem,
):
    space = lax.axis_index("space")
    spaces = lax.axis_size("space")
    shot = lax.axis_index("shot")
    shots = lax.axis_size("shot")
    cells_x, rows_y, rows_z = out.shape[2:]
    slab = velocity.shape[1]
    flat = (cells_x * rows_y, rows_z)
    has_left = space > 0
    has_right = space < spaces - 1

    load = pltpu.make_async_copy(waves, out, local_sem.at[0])
    load.start()
    load_left = pltpu.make_async_copy(left, left_ref, local_sem.at[2])
    load_left.start()
    load_right = pltpu.make_async_copy(right, right_ref, local_sem.at[3])
    load_right.start()
    own_speed = pltpu.make_async_copy(velocity, speeds.at[shot], local_sem.at[1])
    own_speed.start()

    barrier = pltpu.get_barrier_semaphore()

    @pl.when(has_left)
    def _():
        pl.semaphore_signal(barrier, inc=1, device_id={"space": space - 1}, device_id_type=pl.DeviceIdType.MESH)

    @pl.when(has_right)
    def _():
        pl.semaphore_signal(barrier, inc=1, device_id={"space": space + 1}, device_id_type=pl.DeviceIdType.MESH)

    for ahead in range(1, shots):
        peer = lax.rem(shot + ahead, shots)
        pl.semaphore_signal(barrier, inc=1, device_id={"shot": peer}, device_id_type=pl.DeviceIdType.MESH)
    pl.semaphore_wait(barrier, shots - 1 + jnp.where(has_left, 1, 0) + jnp.where(has_right, 1, 0))

    def to_right(source, slot, field):
        return pltpu.make_async_remote_copy(
            source.at[field, cells_x - REACH : cells_x],
            halo.at[slot, field, 0],
            halo_send.at[slot, field, 0],
            halo_recv.at[slot, field, 0],
            device_id={"space": space + 1},
            device_id_type=pl.DeviceIdType.MESH,
        )

    def to_left(source, slot, field):
        return pltpu.make_async_remote_copy(
            source.at[field, 0:REACH],
            halo.at[slot, field, 1],
            halo_send.at[slot, field, 1],
            halo_recv.at[slot, field, 1],
            device_id={"space": space - 1},
            device_id_type=pl.DeviceIdType.MESH,
        )

    def send(source, slot, field, side):
        if side == 0:
            @pl.when(has_left)
            def _():
                to_left(source, slot, field).start()
        else:
            @pl.when(has_right)
            def _():
                to_right(source, slot, field).start()

    def sent(source, slot, field):
        @pl.when(has_right)
        def _():
            to_right(source, slot, field).wait_send()

        @pl.when(has_left)
        def _():
            to_left(source, slot, field).wait_send()

    def received(source, slot, field, side):
        if side == 0:
            @pl.when(has_left)
            def _():
                to_right(source, slot, field).wait_recv()
        else:
            @pl.when(has_right)
            def _():
                to_left(source, slot, field).wait_recv()

    for field in range(2):
        for side in range(2):
            send(waves.at[1], 0, field, side)

    speed_copies = []
    for ahead in range(1, shots):
        peer = lax.rem(shot + ahead, shots)
        copy = pltpu.make_async_remote_copy(
            velocity,
            speeds.at[shot],
            speed_send.at[ahead - 1],
            speed_recv.at[ahead - 1],
            device_id={"shot": peer},
            device_id_type=pl.DeviceIdType.MESH,
        )
        copy.start()
        speed_copies.append(copy)

    @pl.when(jnp.logical_not(has_left))
    def _():
        halo[:, :, 0] = jnp.zeros((STEPS, 2, REACH, rows_y, rows_z), jnp.float32)

    @pl.when(jnp.logical_not(has_right))
    def _():
        halo[:, :, 1] = jnp.zeros((STEPS, 2, REACH, rows_y, rows_z), jnp.float32)

    total[...] = jnp.zeros(total.shape, jnp.float32)
    global_x = space * cells_x + lax.broadcasted_iota(jnp.int32, inside.shape, 0)
    within = (global_x >= aperture[0, 0]) & (global_x < aperture[0, 1])
    inside[...] = jnp.where(within, 1.0, 0.0)

    def spread(now, field):
        cells = out[now, field].reshape(flat)
        high = cells.astype(jnp.bfloat16)
        low = (cells - high.astype(jnp.float32)).astype(jnp.bfloat16)
        lap[field] = (
            jnp.dot(left_ref[...], jnp.concatenate([high, low, high], axis=0), preferred_element_type=jnp.float32)
            + jnp.dot(jnp.concatenate([high, low, high], axis=1), right_ref[...], preferred_element_type=jnp.float32)
            + (3.0 * coefficients[0]) * cells
        ).reshape(lap.shape[1:])

    def advance(now, then, field, start, stop, beside=None):
        cells = slice(start, stop)
        summed = lap[field, cells]
        if beside is not None:
            summed = summed + beside
        following = (
            inside[cells] * (2.0 * out[now, field, cells] - out[then, field, cells])
            + speed[cells] * summed
        )
        out[then, field, cells] = following
        if field == 1:
            total[cells] = total[cells] + out[then, 0, cells] * following

    def border(index, now, then, field, side):
        received(out.at[now], index, field, side)
        for cell in range(REACH):
            if side == 0:
                at = cell
                beside = sum(
                    coefficients[cell + REACH - layer] * halo[index, field, 0, layer]
                    for layer in range(cell, REACH)
                )
            else:
                at = cells_x - REACH + cell
                beside = sum(
                    coefficients[REACH + layer - cell] * halo[index, field, 1, layer]
                    for layer in range(cell + 1)
                )
            advance(now, then, field, at, at + 1, beside[None])

    def step(index, carry):
        then = lax.rem(index, 2)
        now = 1 - then
        for field in range(2):
            @pl.when(index > 1)
            def _():
                sent(out.at[then], index - 1, field)

            @pl.when(index == 1)
            def _():
                sent(waves.at[1], 0, field)

            advance(now, then, field, REACH, cells_x - REACH)
            for side in range(2):
                border(index, now, then, field, side)
                send(out.at[then], index + 1, field, side)
            spread(then, field)
        return carry

    load.wait()
    load_left.wait()
    load_right.wait()
    spread(1, 0)
    spread(1, 1)
    own_speed.wait()
    for copy in speed_copies:
        copy.wait()
    for index in range(shots):
        rows = slice(index * slab, (index + 1) * slab)
        speed[:, rows, :] = speeds[index]
    speed[...] = speed[...] * inside[...]

    lax.fori_loop(0, STEPS - 1, step, 0)

    last = STEPS - 1
    then = last % 2
    now = 1 - then
    keep_now = pltpu.make_async_copy(out.at[now], finals.at[0], local_sem.at[0])
    keep_now.start()

    def part_copy(kind, source, target, ahead):
        peer = lax.rem(shot + ahead, shots)
        return pltpu.make_async_remote_copy(
            source.at[peer],
            target.at[ahead - 1],
            part_send.at[kind, ahead - 1],
            part_recv.at[kind, ahead - 1],
            device_id={"shot": peer},
            device_id_type=pl.DeviceIdType.MESH,
        )

    for field in range(2):
        sent(out.at[then], last - 1, field)
        advance(now, then, field, REACH, cells_x - REACH)
    for index in range(shots):
        rows = slice(index * slab, (index + 1) * slab)
        middle[index] = total[REACH : cells_x - REACH, rows, :]
    copies = [part_copy(0, middle, middle_arrived, ahead) for ahead in range(1, shots)]
    for copy in copies:
        copy.start()
    for field in range(2):
        for side in range(2):
            border(last, now, then, field, side)
    for index in range(shots):
        rows = slice(index * slab, (index + 1) * slab)
        edges[index, 0:REACH] = total[0:REACH, rows, :]
        edges[index, REACH:] = total[cells_x - REACH :, rows, :]
    edge_copies = [part_copy(1, edges, edges_arrived, ahead) for ahead in range(1, shots)]
    for copy in edge_copies:
        copy.start()
    keep_then = pltpu.make_async_copy(out.at[then], finals.at[1], local_sem.at[1])
    keep_then.start()
    for field in range(2):
        sent(out.at[now], last, field)
    summed = middle[shot]
    for copy, ahead in zip(copies, range(1, shots)):
        copy.wait()
        summed = summed + middle_arrived[ahead - 1]
    image[REACH : cells_x - REACH] = summed / STEPS
    summed = edges[shot]
    for copy, ahead in zip(edge_copies, range(1, shots)):
        copy.wait()
        summed = summed + edges_arrived[ahead - 1]
    image[0:REACH] = summed[0:REACH] / STEPS
    image[cells_x - REACH :] = summed[REACH:] / STEPS
    keep_now.wait()
    keep_then.wait()


def keep(fields, image, fields_out, image_out, fields_held, image_held, load_sem, store_sem):
    pieces = [(image, image_held, image_out)]
    for time in range(2):
        for field in range(2):
            pieces.append(
                (fields.at[time, field], fields_held.at[time, field], fields_out.at[time, field])
            )
    loads = [
        pltpu.make_async_copy(source, held, load_sem.at[at])
        for at, (source, held, _) in enumerate(pieces)
    ]
    stores = [
        pltpu.make_async_copy(held, target, store_sem.at[at])
        for at, (_, held, target) in enumerate(pieces)
    ]
    for load in loads:
        load.start()
    for load, store in zip(loads, stores):
        load.wait()
        store.start()
    for store in stores:
        store.wait()


def shards(wavefields, velocity, aperture):
    fields = wavefields[0]
    cells_x, rows_y, rows_z = fields.shape[2:]
    shots = lax.axis_size("shot")
    slab = velocity.shape[1]
    left = split(
        np.kron(band(cells_x), np.eye(rows_y, dtype=np.float32))
        + np.kron(np.eye(cells_x, dtype=np.float32), band(rows_y)),
        1,
    )
    right = split(band(rows_z), 0)
    grid = (cells_x, rows_y, rows_z)
    vmem = pl.BlockSpec(memory_space=pltpu.VMEM)
    anywhere = pl.BlockSpec(memory_space=pl.ANY)
    finals, image = pl.pallas_call(
        kernel,
        out_shape=(
            jax.ShapeDtypeStruct(fields.shape, jnp.float32),
            jax.ShapeDtypeStruct(velocity.shape, jnp.float32),
        ),
        in_specs=[anywhere, anywhere, anywhere, anywhere, pl.BlockSpec(memory_space=pltpu.SMEM)],
        out_specs=(anywhere, vmem),
        scratch_shapes=[
            pltpu.VMEM(left.shape, jnp.bfloat16),
            pltpu.VMEM(right.shape, jnp.bfloat16),
            pltpu.VMEM(fields.shape, jnp.float32),
            pltpu.VMEM((STEPS, 2, 2, REACH, rows_y, rows_z), jnp.float32),
            pltpu.VMEM((shots,) + velocity.shape, jnp.float32),
            pltpu.VMEM(grid, jnp.float32),
            pltpu.VMEM(grid, jnp.float32),
            pltpu.VMEM((2,) + grid, jnp.float32),
            pltpu.VMEM(grid, jnp.float32),
            pltpu.VMEM((shots, cells_x - 2 * REACH, slab, rows_z), jnp.float32),
            pltpu.VMEM((shots - 1, cells_x - 2 * REACH, slab, rows_z), jnp.float32),
            pltpu.VMEM((shots, 2 * REACH, slab, rows_z), jnp.float32),
            pltpu.VMEM((shots - 1, 2 * REACH, slab, rows_z), jnp.float32),
            pltpu.SemaphoreType.DMA((STEPS, 2, 2)),
            pltpu.SemaphoreType.DMA((STEPS, 2, 2)),
            pltpu.SemaphoreType.DMA((shots - 1,)),
            pltpu.SemaphoreType.DMA((shots - 1,)),
            pltpu.SemaphoreType.DMA((2, shots - 1)),
            pltpu.SemaphoreType.DMA((2, shots - 1)),
            pltpu.SemaphoreType.DMA((4,)),
        ],
        compiler_params=pltpu.CompilerParams(collective_id=0, has_side_effects=True),
    )(jnp.asarray(left), jnp.asarray(right), fields, velocity, aperture)
    finals, image = pl.pallas_call(
        keep,
        out_shape=(
            jax.ShapeDtypeStruct(fields.shape, jnp.float32),
            jax.ShapeDtypeStruct(velocity.shape, jnp.float32),
        ),
        in_specs=[anywhere, anywhere],
        out_specs=(anywhere, anywhere),
        scratch_shapes=[
            pltpu.VMEM(fields.shape, jnp.float32),
            pltpu.VMEM(velocity.shape, jnp.float32),
            pltpu.SemaphoreType.DMA((5,)),
            pltpu.SemaphoreType.DMA((5,)),
        ],
    )(finals, image)
    return finals[None], image


def solution(mesh):
    in_specs = (
        P(("groups", "shot"), None, None, "space", None, None),
        P(("groups", "space"), "shot", None),
        P(("groups", "shot"), None),
    )
    out_specs = (
        P(("groups", "shot"), None, None, "space", None, None),
        P(("groups", "space"), "shot", None),
    )
    return jax.shard_map(shards, mesh=mesh, in_specs=in_specs, out_specs=out_specs, check_vma=False)
```

time: 46.5 us -> 43.6 us (0.938)
  local copies, waits for them, and re-layouts: 2.93 us -> 0 us
    unnamed x4 -> x0, local copies, waits for them, and re-layouts: 2.93 us -> none
    pallas_call x0 -> x1, Pallas kernels: none -> 2.04 us  [shards(): pl.pallas_call(keep, out_shape=(jax.ShapeDtypeStruct(fields.shape, jnp.fl...]
    pallas_call x1, Pallas kernels: 42.7 us -> 40.8 us  [shards(): pl.pallas_call(kernel, out_shape=(jax.ShapeDtypeStruct(fields.shape, jnp....]
where the time goes in v2:
time: 43.6 us; the launch traced here: 43.5 us
  Pallas kernels  42.8 us (98%)
  between operations  0.64 us (1%)
    pallas_call x1, Pallas kernels, shards(): pl.pallas_call(kernel, out_shape=(jax.ShapeDtypeStruct(fields.shape, jnp....  40.8 us
    pallas_call x1, Pallas kernels, shards(): pl.pallas_call(keep, out_shape=(jax.ShapeDtypeStruct(fields.shape, jnp.fl...  2.04 us

profile of v2, /device:TPU:0, one launch (start us, length us, event | category | flops | bytes accessed | tf_op | source)
XLA Modules:
  0.0 43.5 jit_solution(8818772074759710221)
XLA Ops:
  0.6 40.8 %shard_map.68 = (f32[2,2,16,16,256]{4,3,2,1,0:T(8,128)}, f32[16,4,256]{2,1,0:T(4,128)}) custom-call(bf16[256,768]{1,0:T(8,128)(2,1)} %constant.4.clone.left, bf16[768,256]{1,0:T(8,128)(2,1)} %constant.5.clone.right, f32[2,2,16,16,256]{4,3,2,1,0:T(8,128)} %bitcast.2, f32[16,4,256]{2,1,0:T(4,128)} %velocity.1, s32[1,2]{1,0:T(1,128)} %aperture.1), custom_call_target="tpu_custom_call" | custom-call | tf_op jit(solution)/shard_map/pallas_call | solution.py:320
  41.4 2.0 %shard_map.69 = (f32[2,2,16,16,256]{4,3,2,1,0:T(8,128)}, f32[16,4,256]{2,1,0:T(4,128)}) custom-call(f32[2,2,16,16,256]{4,3,2,1,0:T(8,128)} %get-tuple-element.6.fields, f32[16,4,256]{2,1,0:T(4,128)} %get-tuple-element.7.image), custom_call_target="tpu_custom_call" | custom-call | tf_op jit(solution)/shard_map/pallas_call | solution.py:352

commit v3 on v2

--- a/solution.py
+++ b/solution.py
@@ -123,19 +123,31 @@
         for side in range(2):
             send(waves.at[1], 0, field, side)
 
+    spans = ((0, REACH), (cells_x - REACH, cells_x), (REACH, cells_x - REACH))
     speed_copies = []
-    for ahead in range(1, shots):
-        peer = lax.rem(shot + ahead, shots)
-        copy = pltpu.make_async_remote_copy(
-            velocity,
-            speeds.at[shot],
-            speed_send.at[ahead - 1],
-            speed_recv.at[ahead - 1],
-            device_id={"shot": peer},
-            device_id_type=pl.DeviceIdType.MESH,
-        )
-        copy.start()
-        speed_copies.append(copy)
+    for kind, (start, stop) in enumerate(spans):
+        for ahead in range(1, shots):
+            peer = lax.rem(shot + ahead, shots)
+            copy = pltpu.make_async_remote_copy(
+                velocity.at[start:stop],
+                speeds.at[shot, start:stop],
+                speed_send.at[kind, ahead - 1],
+                speed_recv.at[kind, ahead - 1],
+                device_id={"shot": peer},
+                device_id_type=pl.DeviceIdType.MESH,
+            )
+            copy.start()
+            speed_copies.append(copy)
+
+    def gather(kinds):
+        for kind in kinds:
+            start, stop = spans[kind]
+            for copy in speed_copies[kind * (shots - 1) : (kind + 1) * (shots - 1)]:
+                copy.wait()
+            for index in range(shots):
+                rows = slice(index * slab, (index + 1) * slab)
+                speed[start:stop, rows, :] = speeds[index, start:stop]
+            speed[start:stop] = speed[start:stop] * inside[start:stop]
 
     @pl.when(jnp.logical_not(has_left))
     def _():
@@ -215,14 +227,17 @@
     spread(1, 0)
     spread(1, 1)
     own_speed.wait()
-    for copy in speed_copies:
-        copy.wait()
-    for index in range(shots):
-        rows = slice(index * slab, (index + 1) * slab)
-        speed[:, rows, :] = speeds[index]
-    speed[...] = speed[...] * inside[...]
-
-    lax.fori_loop(0, STEPS - 1, step, 0)
+    gather((0, 1))
+    for field in range(2):
+        for side in range(2):
+            border(0, 1, 0, field, side)
+            send(out.at[0], 1, field, side)
+    gather((2,))
+    for field in range(2):
+        advance(1, 0, field, REACH, cells_x - REACH)
+        spread(0, field)
+
+    lax.fori_loop(1, STEPS - 1, step, 0)
 
     last = STEPS - 1
     then = last % 2
@@ -341,8 +356,8 @@
             pltpu.VMEM((shots - 1, 2 * REACH, slab, rows_z), jnp.float32),
             pltpu.SemaphoreType.DMA((STEPS, 2, 2)),
             pltpu.SemaphoreType.DMA((STEPS, 2, 2)),
-            pltpu.SemaphoreType.DMA((shots - 1,)),
-            pltpu.SemaphoreType.DMA((shots - 1,)),
+            pltpu.SemaphoreType.DMA((3, shots - 1)),
+            pltpu.SemaphoreType.DMA((3, shots - 1)),
             pltpu.SemaphoreType.DMA((2, shots - 1)),
             pltpu.SemaphoreType.DMA((2, shots - 1)),
             pltpu.SemaphoreType.DMA((4,)),

time: 43.6 us -> 42.8 us (0.982)
  Pallas kernels: 42.8 us -> 42 us
    pallas_call x1, Pallas kernels: 40.8 us -> 40 us  [shards(): pl.pallas_call(kernel, out_shape=(jax.ShapeDtypeStruct(fields.shape, jnp....]
where the time goes in v3:
time: 42.8 us; the launch traced here: 42.7 us
  Pallas kernels  42 us (98%)
  between operations  0.64 us (1%)
    pallas_call x1, Pallas kernels, shards(): pl.pallas_call(kernel, out_shape=(jax.ShapeDtypeStruct(fields.shape, jnp....  40 us
    pallas_call x1, Pallas kernels, shards(): pl.pallas_call(keep, out_shape=(jax.ShapeDtypeStruct(fields.shape, jnp.fl...  2.04 us

profile of v3, /device:TPU:0, one launch (start us, length us, event | category | flops | bytes accessed | tf_op | source)
XLA Modules:
  0.0 42.7 jit_solution(4364980037182871177)
XLA Ops:
  0.6 40.0 %shard_map.68 = (f32[2,2,16,16,256]{4,3,2,1,0:T(8,128)}, f32[16,4,256]{2,1,0:T(4,128)}) custom-call(bf16[256,768]{1,0:T(8,128)(2,1)} %constant.4.clone.left, bf16[768,256]{1,0:T(8,128)(2,1)} %constant.5.clone.right, f32[2,2,16,16,256]{4,3,2,1,0:T(8,128)} %bitcast.2, f32[16,4,256]{2,1,0:T(4,128)} %velocity.1, s32[1,2]{1,0:T(1,128)} %aperture.1), custom_call_target="tpu_custom_call" | custom-call | tf_op jit(solution)/shard_map/pallas_call | solution.py:335
  40.6 2.0 %shard_map.69 = (f32[2,2,16,16,256]{4,3,2,1,0:T(8,128)}, f32[16,4,256]{2,1,0:T(4,128)}) custom-call(f32[2,2,16,16,256]{4,3,2,1,0:T(8,128)} %get-tuple-element.6.fields, f32[16,4,256]{2,1,0:T(4,128)} %get-tuple-element.7.image), custom_call_target="tpu_custom_call" | custom-call | tf_op jit(solution)/shard_map/pallas_call | solution.py:367

commit v4 on v3

--- a/solution.py
+++ b/solution.py
@@ -214,10 +214,10 @@
             def _():
                 sent(waves.at[1], 0, field)
 
-            advance(now, then, field, REACH, cells_x - REACH)
             for side in range(2):
                 border(index, now, then, field, side)
                 send(out.at[then], index + 1, field, side)
+            advance(now, then, field, REACH, cells_x - REACH)
             spread(then, field)
         return carry
 

time: 42.8 us -> 42.8 us (level)
  no operation moved by 1% of the time
where the time goes in v4:
time: 42.8 us; the launch traced here: 42.7 us
  Pallas kernels  42.1 us (98%)
  between operations  0.64 us (1%)
    pallas_call x1, Pallas kernels, shards(): pl.pallas_call(kernel, out_shape=(jax.ShapeDtypeStruct(fields.shape, jnp....  40 us
    pallas_call x1, Pallas kernels, shards(): pl.pallas_call(keep, out_shape=(jax.ShapeDtypeStruct(fields.shape, jnp.fl...  2.04 us

profile of v4, /device:TPU:0, one launch (start us, length us, event | category | flops | bytes accessed | tf_op | source)
XLA Modules:
  0.0 42.7 jit_solution(12192063535867343063)
XLA Ops:
  0.6 40.0 %shard_map.68 = (f32[2,2,16,16,256]{4,3,2,1,0:T(8,128)}, f32[16,4,256]{2,1,0:T(4,128)}) custom-call(bf16[256,768]{1,0:T(8,128)(2,1)} %constant.4.clone.left, bf16[768,256]{1,0:T(8,128)(2,1)} %constant.5.clone.right, f32[2,2,16,16,256]{4,3,2,1,0:T(8,128)} %bitcast.2, f32[16,4,256]{2,1,0:T(4,128)} %velocity.1, s32[1,2]{1,0:T(1,128)} %aperture.1), custom_call_target="tpu_custom_call" | custom-call | tf_op jit(solution)/shard_map/pallas_call | solution.py:335
  40.7 2.0 %shard_map.69 = (f32[2,2,16,16,256]{4,3,2,1,0:T(8,128)}, f32[16,4,256]{2,1,0:T(4,128)}) custom-call(f32[2,2,16,16,256]{4,3,2,1,0:T(8,128)} %get-tuple-element.6.fields, f32[16,4,256]{2,1,0:T(4,128)} %get-tuple-element.7.image), custom_call_target="tpu_custom_call" | custom-call | tf_op jit(solution)/shard_map/pallas_call | solution.py:367
